TPU v7x, 32 devices: a whole 2x2x4 slice. The times are simulated.
32 devices in a mesh: ga: 2 (over y), ea: 16 (over z, x, core).
Axes of the slice: x: 2, y: 2, z: 4, core: 2. Of those that a mesh axis runs over, the one named last changes fastest.
Arguments:
- tokens: bfloat16 [4096, 2048], P(('ga', 'ea')), parts along dimension 0, may hold values from -6 to 6
- expert_choice_index: int32 [4096, 4], P(('ga', 'ea')), parts along dimension 0, may hold values from 0 to 7, all different within a row; in each aligned block of 128 rows (0 to 127, 128 to 255, ...) at most 72 rows name the same one
- router_gate_weight: float32 [4096, 4], P(('ga', 'ea')), parts along dimension 0, may hold values from 0.05 to 0.6
- cotangent: bfloat16 [4096, 2048], P(('ga', 'ea')), parts along dimension 0, may hold values from -6 to 6
- gate_up_matrix: bfloat16 [16, 2048, 1408], P('ea'), may hold values from -0.125 to 0.125
- down_weight: bfloat16 [16, 704, 2048], P('ea'), may hold values from -0.15625 to 0.15625
- adapter_input_projection: bfloat16 [2048, 16], replicated, may hold values from -0.125 to 0.125
- adapter_output_projection: bfloat16 [16, 16, 1408], P('ea'), may hold values from -0.59765625 to 0.59765625
Outputs:
- layer_output: bfloat16 [4096, 2048], P(('ga', 'ea')), parts along dimension 0
- adapter_input_gradient: float32 [4096, 16], P('ga'), parts along dimension 0
- lora_b_grad: float32 [32, 16, 1408], P(('ga', 'ea')), parts along dimension 0
There are 2 independent parts, one for each index of `ga`. A program takes and returns all parts, laid end to end along the dimension named above; an argument that names none is the same for every part. Nothing has to cross between parts.
Inputs may be any that keep to these rules, and one draw needn't show every extreme that they name: `expert_choice_index`: each row names 4 different experts. Within the rows of one device (aligned blocks of 128 rows) no expert is named by more than 72 rows, and in every draw some expert is named by exactly 72 rows of some block.
All inputs are finite; a program needn't handle non-finite values.
Results may differ from a plain program's by a relative error of at most 0.0072.
Values may be sent and summed in bfloat16 or wider, within the bound.
A program may use at most 128 MiB of HBM per device.

v0:
```python
import jax
import jax.numpy as jnp
from jax import lax
from jax.sharding import PartitionSpec as P

EXPERT_SPLIT = 2


adapter_scale = 2.0


def from_partner(value, axis, distance):
    mask = 2**distance
    pairs = [(source, source ^ mask) for source in range(lax.axis_size(axis))]
    return lax.ppermute(value, axis, pairs)


def slot_ranks(id_block, experts):
    flat_ids = id_block.reshape(-1)
    onehot = (flat_ids[:, None] == jnp.arange(experts, dtype=jnp.int32)[None, :]).astype(jnp.int32)
    before = jnp.cumsum(onehot, axis=0) - onehot
    return jnp.sum(before * onehot, axis=1).reshape(id_block.shape)


def block_halfway(
    input_rows, output_gradient_rows, gate_up_weight, down_w, adapter_a, adapter_output_weight
):
    adapter_input_rows = jnp.dot(input_rows, adapter_a, preferred_element_type=jnp.float32).astype(
        jnp.bfloat16
    )
    joined_columns = jnp.dot(
        input_rows, gate_up_weight, preferred_element_type=jnp.float32
    ) + adapter_scale * jnp.dot(
        adapter_input_rows, adapter_output_weight, preferred_element_type=jnp.float32
    )
    block_width = down_w.shape[0]
    gate_part = joined_columns[:, :block_width]
    up_part = joined_columns[:, block_width:]
    sigmoid_gate = jax.nn.sigmoid(gate_part)
    active = gate_part * sigmoid_gate
    hidden = (active * up_part).astype(jnp.bfloat16)
    partial_value = jnp.dot(hidden, down_w, preferred_element_type=jnp.float32).astype(jnp.bfloat16)
    down_grad = lax.dot_general(
        output_gradient_rows, down_w, (((1,), (1,)), ((), ())), preferred_element_type=jnp.float32
    )
    gate_grad = down_grad * up_part * sigmoid_gate * (1.0 + gate_part * (1.0 - sigmoid_gate))
    up_grad = down_grad * active
    joined_gradient = jnp.concatenate([gate_grad, up_grad], axis=1).astype(jnp.bfloat16)
    output_gradient_part = adapter_scale * lax.dot_general(
        adapter_input_rows,
        joined_gradient,
        (((0,), (0,)), ((), ())),
        preferred_element_type=jnp.float32,
    )
    adapter_gradient = (
        adapter_scale
        * lax.dot_general(
            joined_gradient,
            adapter_output_weight,
            (((1,), (1,)), ((), ())),
            preferred_element_type=jnp.float32,
        )
    ).astype(jnp.bfloat16)
    grad_a = lax.dot_general(
        input_rows, adapter_gradient, (((0,), (0,)), ((), ())), preferred_element_type=jnp.float32
    )
    return (partial_value, grad_a, output_gradient_part)


def local(
    tokens,
    expert_choice_index,
    router_gate_weight,
    cotangent,
    gate_up_matrix,
    down_weight,
    adapter_input_projection,
    adapter_output_projection,
):
    devices = lax.axis_size("ea")
    experts = devices // EXPERT_SPLIT
    tok_rows, model_width = tokens.shape
    top_count = expert_choice_index.shape[1]
    capacity = 9 * tok_rows * top_count // (8 * experts)
    half_width = model_width // 2
    parity = lax.axis_index("ea") % 2
    slot_rank = slot_ranks(expert_choice_index, experts)
    slot_rows = (expert_choice_index * capacity + slot_rank).reshape(-1)
    scaled_dy = (router_gate_weight[:, :, None] * cotangent[:, None, :].astype(jnp.float32)).astype(
        jnp.bfloat16
    )
    repeated = jnp.broadcast_to(tokens[:, None, :], (tok_rows, top_count, model_width))
    both_rows = jnp.stack([repeated, scaled_dy], axis=2).reshape(
        tok_rows * top_count, 2, model_width
    )
    blank_rows = jnp.zeros((experts * capacity, 2, model_width), jnp.bfloat16)
    send_rows = blank_rows.at[slot_rows].set(both_rows, unique_indices=True)
    rows_total = devices * capacity
    halves = (
        send_rows.reshape(experts, capacity, 2, 2, half_width)
        .transpose(0, 3, 1, 2, 4)
        .reshape(devices, capacity, 2, half_width)
    )
    own_piece = lax.all_to_all(halves, "ea", split_axis=0, concat_axis=0, tiled=True)
    other_piece = from_partner(own_piece, "ea", 0)
    lower_block_part = jnp.where(parity == 0, own_piece, other_piece)
    upper_block_part = jnp.where(parity == 0, other_piece, own_piece)
    arrived = jnp.concatenate([lower_block_part, upper_block_part], axis=3)
    input_rows = arrived[:, :, 0].reshape(rows_total, model_width)
    output_gradient_rows = arrived[:, :, 1].reshape(rows_total, model_width)
    partial_value, input_gradient_local, output_gradient_part = block_halfway(
        input_rows,
        output_gradient_rows,
        gate_up_matrix[0],
        down_weight[0],
        adapter_input_projection,
        adapter_output_projection[0],
    )
    adapter_input_gradient = lax.psum(input_gradient_local, "ea")
    partial_value = partial_value.reshape(devices, capacity, model_width)
    kept_part = jnp.where(
        parity == 0, partial_value[:, :, :half_width], partial_value[:, :, half_width:]
    )
    given_part = jnp.where(
        parity == 0, partial_value[:, :, half_width:], partial_value[:, :, :half_width]
    )
    taken_part = from_partner(given_part, "ea", 0)
    summed = (kept_part.astype(jnp.float32) + taken_part.astype(jnp.float32)).astype(jnp.bfloat16)
    returned = lax.all_to_all(summed, "ea", split_axis=0, concat_axis=0, tiled=True)
    expert_out = (
        returned.reshape(experts, 2, capacity, half_width)
        .transpose(0, 2, 1, 3)
        .reshape(experts * capacity, model_width)
    )
    picked = expert_out[slot_rows].reshape(tok_rows, top_count, model_width).astype(jnp.float32)
    layer_output = jnp.sum(router_gate_weight[:, :, None] * picked, axis=1).astype(jnp.bfloat16)
    return (layer_output, adapter_input_gradient, output_gradient_part[None])


def shared_local(
    tokens,
    expert_choice_index,
    router_gate_weight,
    cotangent,
    gate_up_matrix,
    down_weight,
    adapter_input_projection,
    adapter_output_projection,
):
    devices = lax.axis_size("ea")
    experts = devices // EXPERT_SPLIT
    tok_rows, model_width = tokens.shape
    top_count = expert_choice_index.shape[1]
    capacity = 9 * tok_rows * top_count // (8 * experts)
    rows_total = devices * capacity
    mine = lax.axis_index("ea") // EXPERT_SPLIT
    block_width = down_weight.shape[1]
    adapter_a = adapter_input_projection
    gate_up_weight, down_w, adapter_out = gate_up_matrix[0], down_weight[0], adapter_output_projection[0]

    choice = lax.all_gather(
        jnp.concatenate([expert_choice_index.astype(jnp.float32), router_gate_weight], axis=1), "ea"
    )
    all_tokens = lax.all_gather(tokens, "ea")
    all_cotangent = lax.all_gather(cotangent, "ea")
    named = choice[:, :, :top_count].astype(jnp.int32) == mine
    weight = jnp.sum(jnp.where(named, choice[:, :, top_count:], 0.0), axis=2)
    chosen = jnp.any(named, axis=2)
    place = jnp.cumsum(chosen.astype(jnp.int32), axis=1) - 1
    place = jnp.where(chosen, place, capacity)
    pick = place[:, None, :] == jnp.arange(capacity, dtype=jnp.int32)[None, :, None]
    select = pick.astype(jnp.bfloat16)
    row_weight = jnp.sum(jnp.where(pick, weight[:, None, :], 0.0), axis=2)

    input_rows = jnp.einsum(
        "sct,std->scd", select, all_tokens, preferred_element_type=jnp.bfloat16
    ).reshape(rows_total, model_width)
    adapter_rows = jnp.dot(input_rows, adapter_a, preferred_element_type=jnp.float32).astype(jnp.bfloat16)
    joined = jnp.dot(
        input_rows, gate_up_weight, preferred_element_type=jnp.float32
    ) + adapter_scale * jnp.dot(adapter_rows, adapter_out, preferred_element_type=jnp.float32)
    gate_part, up_part = joined[:, :block_width], joined[:, block_width:]
    sigmoid_gate = jax.nn.sigmoid(gate_part)
    active = gate_part * sigmoid_gate
    hidden = (active * up_part).astype(jnp.bfloat16)
    partial_value = jnp.dot(hidden, down_w, preferred_element_type=jnp.float32).astype(jnp.bfloat16)
    spread = jnp.einsum(
        "sct,scd->std",
        select,
        partial_value.reshape(devices, capacity, model_width),
        preferred_element_type=jnp.float32,
    )
    term = (weight[:, :, None] * spread).astype(jnp.bfloat16).reshape(devices * tok_rows, model_width)
    layer_output = lax.psum_scatter(term, "ea", scatter_dimension=0, tiled=True)

    gradient_rows = jnp.einsum(
        "sct,std->scd", select, all_cotangent, preferred_element_type=jnp.float32
    )
    gradient_rows = (
        (row_weight[:, :, None] * gradient_rows).astype(jnp.bfloat16).reshape(rows_total, model_width)
    )
    down_grad = lax.dot_general(
        gradient_rows, down_w, (((1,), (1,)), ((), ())), preferred_element_type=jnp.float32
    )
    gate_grad = down_grad * up_part * sigmoid_gate * (1.0 + gate_part * (1.0 - sigmoid_gate))
    up_grad = down_grad * active
    joined_gradient = jnp.concatenate([gate_grad, up_grad], axis=1).astype(jnp.bfloat16)
    lora_b = adapter_scale * lax.dot_general(
        adapter_rows, joined_gradient, (((0,), (0,)), ((), ())), preferred_element_type=jnp.float32
    )
    adapter_gradient = (
        adapter_scale
        * lax.dot_general(
            joined_gradient, adapter_out, (((1,), (1,)), ((), ())), preferred_element_type=jnp.float32
        )
    ).astype(jnp.bfloat16)
    grad_a = lax.dot_general(
        input_rows, adapter_gradient, (((0,), (0,)), ((), ())), preferred_element_type=jnp.float32
    )
    return (layer_output, lax.psum(grad_a, "ea"), lora_b[None])


def solution(mesh):
    in_specs = (
        P(("ga", "ea"), None),
        P(("ga", "ea"), None),
        P(("ga", "ea"), None),
        P(("ga", "ea"), None),
        P("ea", None, None),
        P("ea", None, None),
        P(),
        P("ea", None, None),
    )
    out_specs = (P(("ga", "ea"), None), P("ga", None), P(("ga", "ea"), None, None))
    few = mesh.shape["ea"] // EXPERT_SPLIT

    def chosen(*args):
        wide = few > 2 * args[1].shape[1]
        body = local if wide else shared_local
        return jax.shard_map(
            body, mesh=mesh, in_specs=in_specs, out_specs=out_specs, check_vma=False
        )(*args)

    return chosen
```

profile of v0, /device:TPU:0, one launch (start us, length us, event | category | flops | bytes accessed | tf_op | source)
XLA Modules:
  0.0 392.2 jit_solution(9553728436443221169)
XLA Ops:
  7.2 0.0 copy-start
  7.2 0.0 all-gather.6.cloned.1.call-start
  7.2 0.7 all-gather.6.cloned.1.call-update
  7.9 0.0 all-gather.8.cloned.1.call-start
  8.0 0.7 all-gather.8.cloned.1.call-update
  8.7 0.0 all-reduce.2.cloned.1.call-start
  8.7 0.7 convert_element_type.33
  9.4 0.7 pad_maximum_fusion.5
  10.1 23.8 %all-gather = f32[2048,8]{0,1:T(8,128)S(1)} all-gather(f32[128,8]{0,1:T(8,128)S(1)} %pad_maximum_fusion.5), channel_id=2, replica_groups=mesh['ga'=2,'ea'=16] {'ea'}, dimensions={0}, use_global_device_ids=true | all-gather | bytes 69632 | tf_op jit(solution)/shard_map/all_gather | solution.py:161
  33.9 0.3 reduce_window_sum.11
  34.3 0.3 select_reduce_fusion
  34.6 52.7 %all-gather.6.cloned.1.call-done = bf16[2048,2048]{1,0:T(8,128)(2,1)} async-done(((bf16[128,2048]{1,0:T(8,128)(2,1)}), bf16[2048,2048]{1,0:T(8,128)(2,1)}) %all-gather.6.cloned.1.call-update) | async-done | bytes 8388624 | tf_op jit(solution)/shard_map/all_gather | solution.py:164
  87.3 4.8 %fusion.10 = bf16[16,72,2048]{2,1,0:T(8,128)(2,1)S(1)} fusion(bf16[16,128,2048]{2,1,0:T(8,128)(2,1)} %bitcast.40, s32[16,128]{1,0:T(8,128)S(1)} %add_select_fusion), kind=kOutput, calls=%fused_computation.24 | convolution fusion | flops 604127232 | bytes 13115392 | tf_op jit(solution)/shard_map/sct,std->scd/dot_general | solution.py:175
  92.1 0.0 copy-start.1
  92.1 1.3 convolution_convert_fusion.1
  93.5 0.8 copy-done.1
  94.3 11.5 %fusion.1 = f32[1152,1408]{1,0:T(8,128)} fusion(bf16[1152,2048]{1,0:T(8,128)(2,1)S(1)} %bitcast.36, bf16[1,2048,1408]{2,1,0:T(8,128)(2,1)} %param.12), kind=kOutput, calls=%fused_computation.5 | convolution fusion | flops 6643777536 | bytes 16973824 | tf_op jit(solution)/shard_map/dot_general | solution.py:179
  105.8 56.6 %all-gather.8.cloned.1.call-done = bf16[2048,2048]{1,0:T(8,128)(2,1)} async-done(((bf16[128,2048]{1,0:T(8,128)(2,1)}), bf16[2048,2048]{1,0:T(8,128)(2,1)}) %all-gather.8.cloned.1.call-update) | async-done | bytes 8388624 | tf_op jit(solution)/shard_map/all_gather | solution.py:165
  162.4 4.9 %multiply_convert_fusion.1 = bf16[16,72,2048]{2,1,0:T(8,128)(2,1)S(1)} fusion(f32[16,72]{1,0:T(8,128)S(1)} %select_reduce_fusion, bf16[16,128,2048]{2,1,0:T(8,128)(2,1)} %bitcast.39, s32[16,128]{1,0:T(8,128)S(1)} %add_select_fusion), kind=kOutput, calls=%fused_computation.3 | convolution fusion | flops 608845824 | bytes 13120000 | tf_op jit(solution)/shard_map/sct,std->scd/dot_general | solution.py:196
  167.3 0.3 copy-done.2
  167.6 1.1 fusion
  168.7 5.7 %convolution_convert_fusion = bf16[1152,2048]{1,0:T(8,128)(2,1)} fusion(bf16[1,704,2048]{2,1,0:T(8,128)(2,1)S(1)} %copy-done, f32[1152,1408]{1,0:T(8,128)S(1)} %fusion), kind=kOutput, calls=%fused_computation.4 | convolution fusion | flops 3329114112 | bytes 14680064 | tf_op jit(solution)/shard_map/dot_general | solution.py:186
  174.4 6.3 %multiply_convert_fusion.3 = (bf16[1152,704]{1,0:T(8,128)(2,1)}, bf16[1152,704]{1,0:T(8,128)(2,1)}) fusion(f32[1152,1408]{1,0:T(8,128)S(1)} %fusion, bf16[1152,2048]{1,0:T(8,128)(2,1)S(1)} %bitcast.41, bf16[1,704,2048]{2,1,0:T(8,128)(2,1)S(1)} %copy-done), kind=kOutput, calls=%fused_computation.8 | convolution fusion | flops 3332431872 | bytes 17334272 | tf_op jit(solution)/shard_map/dot_general | solution.py:202
  180.7 6.8 %fusion.9 = f32[2048,16]{0,1:T(8,128)} fusion(bf16[1152,2048]{1,0:T(8,128)(2,1)} %bitcast.37, bf16[1152,704]{1,0:T(8,128)(2,1)} %get-tuple-element.6, bf16[1152,704]{1,0:T(8,128)(2,1)} %get-tuple-element.5, bf16[1,16,1408]{2,1,0:T(8,128)(2,1)S(1)} %copy-done.4), kind=kOutput, calls=%fused_computation.21 | convolution fusion | flops 133926912 | bytes 8138752 | tf_op jit(solution)/shard_map/dot_general | solution.py:217
  187.4 0.0 all-reduce.2.cloned.1.call-update
  187.5 0.3 reduce-scatter.2.cloned.1.call-start
  187.7 8.0 %multiply_convert_fusion = bf16[16,128,2048]{2,1,0:T(8,128)(2,1)} fusion(f32[16,128]{1,0:T(8,128)S(1)} %fusion.19, bf16[16,72,2048]{2,1,0:T(8,128)(2,1)} %bitcast.42, s32[16,128]{1,0:T(8,128)S(1)} %add_select_fusion), kind=kOutput, calls=%fused_computation | convolution fusion | flops 612515840 | bytes 13123584 | tf_op jit(solution)/shard_map/sct,scd->std/dot_general | solution.py:187
  195.7 0.0 reduce-scatter.2.cloned.1.call-update
  195.8 3.5 fusion.8
  199.2 75.3 %all-reduce.2.cloned.1.call-done = f32[2048,16]{0,1:T(8,128)} async-done(((f32[2048,16]{0,1:T(8,128)}), f32[2048,16]{0,1:T(8,128)}) %all-reduce.2.cloned.1.call-update) | async-done | bytes 131088 | tf_op jit(solution)/shard_map/psum | solution.py:220
  274.5 109.5 %reduce-scatter.2.cloned.1.call-done = bf16[128,2048]{1,0:T(8,128)(2,1)} async-done(((bf16[2048,2048]{1,0:T(8,128)(2,1)}), bf16[128,2048]{1,0:T(8,128)(2,1)}) %reduce-scatter.2.cloned.1.call-update) | async-done | bytes 524304 | tf_op jit(solution)/shard_map/reduce_scatter | solution.py:194
  384.1 1.6 copy.15
  (10 shorter events, 0.1 us)
Async XLA Ops:
  7.2 161.5 %copy-start = (bf16[1,704,2048]{2,1,0:T(8,128)(2,1)S(1)}, bf16[1,704,2048]{2,1,0:T(8,128)(2,1)}, u32[]{:S(2)}) copy-start(bf16[1,704,2048]{2,1,0:T(8,128)(2,1)} %param.13) | copy-start | bytes 8650756
  7.2 80.1 %all-gather.6.cloned.1.call-start = ((), (), s32[]{:S(2)}) async-start(), calls=%async_computation.3 | async-start | bytes 8912896 | tf_op jit(solution)/shard_map/all_gather | solution.py:164
  7.9 154.5 %all-gather.8.cloned.1.call-start = ((), (), s32[]{:S(2)}) async-start(), calls=%async_computation.4 | async-start | bytes 8912896 | tf_op jit(solution)/shard_map/all_gather | solution.py:165
  8.7 265.9 %all-reduce.2.cloned.1.call-start = ((), (), s32[]{:S(2)}) async-start(), calls=%async_computation.2 | async-start | bytes 262144 | tf_op jit(solution)/shard_map/psum | solution.py:220
  87.3 4.8 %copy-start.3 = (bf16[2048,16]{0,1:T(8,128)(2,1)S(1)}, bf16[2048,16]{0,1:T(8,128)(2,1)}, u32[]{:S(2)}) copy-start(bf16[2048,16]{0,1:T(8,128)(2,1)} %param.14) | copy-start | bytes 196612
  92.1 2.1 copy-start.1
  162.4 5.2 %copy-start.2 = (f32[1152,1408]{1,0:T(8,128)S(1)}, f32[1152,1408]{1,0:T(8,128)}, u32[]{:S(2)}) copy-start(f32[1152,1408]{1,0:T(8,128)} %fusion.1) | copy-start | bytes 19464196
  162.4 5.2 %copy-start.4 = (bf16[1,16,1408]{2,1,0:T(8,128)(2,1)S(1)}, bf16[1,16,1408]{2,1,0:T(8,128)(2,1)}, u32[]{:S(2)}) copy-start(bf16[1,16,1408]{2,1,0:T(8,128)(2,1)} %param.15) | copy-start | bytes 135172
  187.5 196.6 %reduce-scatter.2.cloned.1.call-start = ((), (), s32[]{:S(2)}) async-start(), calls=%async_computation.1 | async-start | bytes 8912896 | tf_op jit(solution)/shard_map/reduce_scatter | solution.py:194
Sparse Core Ops, SparseCore 0:
  10.1 77.1 all-gather.5
  89.5 72.8 all-gather.7
  187.6 86.9 all-reduce.1
  279.0 105.0 reduce-scatter.1
where the time goes:
time: 392 us
  waiting for transfers between devices  296 us (76%)
  matrix products  53.8 us (14%)
  blocking collectives  23.8 us (6%)
  between operations  13.8 us (4%)
    reduce_scatter x1, waiting for transfers between devices, shared_local(): layer_output = lax.psum_scatter(term, 'ea', scatter_dimension=0, tiled=True)  110 us
    psum x1, waiting for transfers between devices, shared_local(): return (layer_output, lax.psum(grad_a, 'ea'), lora_b[None])  75.3 us
    all_gather x1, waiting for transfers between devices, shared_local(): all_cotangent = lax.all_gather(cotangent, 'ea')  56.6 us
    all_gather x1, waiting for transfers between devices, shared_local(): all_tokens = lax.all_gather(tokens, 'ea')  52.7 us
    all_gather x1, blocking collectives, shared_local(): lax.all_gather(jnp.concatenate([expert_choice_index.astype(jnp.float32),...  23.8 us
    dot_general x1, matrix products, shared_local(): jnp.dot(input_rows, gate_up_weight, preferred_element_type=jnp.float32)  11.5 us
    dot_general x1, matrix products, shared_local(): jnp.einsum('sct,scd->std', select, partial_value.reshape(devices, capacit...  8 us
  transfers between devices with their start and end apart: 4, of which 4 were waited for; matrix products, arithmetic and copies ran while one was open for 8% of the time, Pallas kernels for 0%

commit v1 on v0

--- a/solution.py
+++ b/solution.py
@@ -1,9 +1,14 @@
+import functools
+
 import jax
 import jax.numpy as jnp
 from jax import lax
+from jax.experimental import pallas as pl
+from jax.experimental.pallas import tpu as pltpu
 from jax.sharding import PartitionSpec as P
 
 EXPERT_SPLIT = 2
+PLANE = 4
 
 
 adapter_scale = 2.0
@@ -137,7 +142,325 @@
     return (layer_output, adapter_input_gradient, output_gradient_part[None])
 
 
-def shared_local(
+def picks_of(info, expert, top_count, capacity):
+    tok_rows = info.shape[1]
+    named = info[:top_count] == expert.astype(jnp.float32)
+    weight = jnp.sum(jnp.where(named, info[top_count:], 0.0), axis=0, keepdims=True)
+    chosen = jnp.sum(jnp.where(named, 1.0, 0.0), axis=0, keepdims=True)
+    before = lax.broadcasted_iota(jnp.int32, (tok_rows, tok_rows), 0)
+    after = lax.broadcasted_iota(jnp.int32, (tok_rows, tok_rows), 1)
+    ahead = jnp.where(before < after, 1.0, 0.0).astype(jnp.bfloat16)
+    place = jnp.dot(
+        jnp.broadcast_to(chosen, (8, tok_rows)).astype(jnp.bfloat16),
+        ahead,
+        preferred_element_type=jnp.float32,
+    )[:1]
+    place = jnp.where(chosen > 0.0, place, -1.0)
+    slots = lax.broadcasted_iota(jnp.int32, (capacity, tok_rows), 0).astype(jnp.float32)
+    pick = jnp.broadcast_to(place, (capacity, tok_rows)) == slots
+    return pick, weight
+
+
+def remote(source, target, send_sem, recv_sem, device):
+    return pltpu.make_async_remote_copy(
+        src_ref=source,
+        dst_ref=target,
+        send_sem=send_sem,
+        recv_sem=recv_sem,
+        device_id={"ea": device},
+        device_id_type=pl.DeviceIdType.MESH,
+    )
+
+
+def greet(here, plane, planes):
+    barrier = pltpu.get_barrier_semaphore()
+
+    def tell(device):
+        pl.semaphore_signal(
+            barrier, inc=1, device_id={"ea": device}, device_id_type=pl.DeviceIdType.MESH
+        )
+
+    tell(here + 1 - 2 * (here % 2))
+    tell(here + 2 - 4 * ((here // 2) % 2))
+
+    @pl.when(plane > 0)
+    def _():
+        tell(here - PLANE)
+
+    @pl.when(plane < planes - 1)
+    def _():
+        tell(here + PLANE)
+
+    ends = jnp.where(plane > 0, 1, 0) + jnp.where(plane < planes - 1, 1, 0)
+    pl.semaphore_wait(barrier, 2 + ends)
+
+
+def gather_kernel(
+    planes, top_count, capacity,
+    x_ref, c_ref, info_ref,
+    rows_ref, grad_ref, infos_ref,
+    line, infos, staged, load_sem, line_send, line_recv, info_send, info_recv, x_send, x_recv,
+    core_send, core_recv,
+):
+    here = lax.axis_index("ea")
+    plane = here // PLANE
+    mine = here // EXPERT_SPLIT
+    partner = here + 1 - 2 * (here % 2)
+    beside = here + 2 - 4 * ((here // 2) % 2)
+    theirs = beside // EXPERT_SPLIT
+    outs = (rows_ref, grad_ref)
+    loads = [
+        pltpu.make_async_copy(ref, line.at[t, plane], load_sem.at[t])
+        for t, ref in enumerate((x_ref, c_ref))
+    ]
+    for load in loads:
+        load.start()
+    infos[plane] = info_ref[...]
+    greet(here, plane, planes)
+    steps = (PLANE, -PLANE)
+    can = (plane < planes - 1, plane > 0)
+
+    def info_copy(at, way):
+        return remote(
+            infos.at[at], infos.at[at], info_send.at[way, at], info_recv.at[at], here + steps[way]
+        )
+
+    def line_copy(t, at, way):
+        return remote(
+            line.at[t, at], line.at[t, at], line_send.at[t, way, at], line_recv.at[t, at],
+            here + steps[way],
+        )
+
+    def x_copy(t, at):
+        return remote(
+            staged.at[t, at], outs[t].at[planes + at], x_send.at[t, at], x_recv.at[t, at], beside
+        )
+
+    def core_copy(t, slot):
+        return remote(
+            outs[t].at[slot], outs[t].at[2 * planes + slot], core_send.at[t, slot],
+            core_recv.at[t, slot], partner,
+        )
+
+    def begin(make, way):
+        @pl.when(can[way])
+        def _():
+            make().start()
+
+    def handle(at, ways, own):
+        if not own:
+            info_copy(at, 0).wait_recv()
+        for way in ways:
+            begin(lambda: info_copy(at, way), way)
+        info = infos[at]
+        ours, our_weight = picks_of(info, mine, top_count, capacity)
+        others, other_weight = picks_of(info, theirs, top_count, capacity)
+        select = jnp.concatenate(
+            [jnp.where(ours, 1.0, 0.0), jnp.where(others, 1.0, 0.0)], axis=0
+        ).astype(jnp.bfloat16)
+        row_weight = jnp.concatenate(
+            [
+                jnp.sum(jnp.where(ours, our_weight, 0.0), axis=1, keepdims=True),
+                jnp.sum(jnp.where(others, other_weight, 0.0), axis=1, keepdims=True),
+            ],
+            axis=0,
+        )
+        for t in range(2):
+            if own:
+                loads[t].wait()
+            else:
+                line_copy(t, at, 0).wait_recv()
+            for way in ways:
+                begin(lambda: line_copy(t, at, way), way)
+            picked = jnp.dot(select, line[t, at], preferred_element_type=jnp.float32)
+            if t == 1:
+                picked = picked * row_weight
+            picked = picked.astype(jnp.bfloat16)
+            staged[t, at] = picked[capacity:]
+            x_copy(t, at).start()
+            outs[t][at] = picked[:capacity]
+            core_copy(t, at).start()
+
+    def relay(at):
+        for t in range(2):
+            x_copy(t, at).wait_recv()
+            core_copy(t, planes + at).start()
+
+    handle(plane, (0, 1), True)
+    for d in range(1, planes):
+        @pl.when(plane >= d)
+        def _():
+            handle(plane - d, (0,), False)
+
+        @pl.when(plane + d < planes)
+        def _():
+            handle(plane + d, (1,), False)
+
+        if d == 1:
+            relay(plane)
+        else:
+            @pl.when(plane >= d - 1)
+            def _():
+                relay(plane - (d - 1))
+
+            @pl.when(plane + d - 1 < planes)
+            def _():
+                relay(plane + (d - 1))
+
+    @pl.when(plane >= planes - 1)
+    def _():
+        relay(plane - (planes - 1))
+
+    @pl.when(plane + planes - 1 < planes)
+    def _():
+        relay(plane + (planes - 1))
+
+    for at in range(planes):
+        @pl.when((plane >= at) & can[0])
+        def _():
+            info_copy(at, 0).wait_send()
+            for t in range(2):
+                line_copy(t, at, 0).wait_send()
+
+        @pl.when((plane <= at) & can[1])
+        def _():
+            info_copy(at, 1).wait_send()
+            for t in range(2):
+                line_copy(t, at, 1).wait_send()
+
+        for t in range(2):
+            x_copy(t, at).wait_send()
+    for t in range(2):
+        for slot in range(2 * planes):
+            core_copy(t, slot).wait()
+    infos_ref[...] = infos[...]
+
+
+def return_kernel(
+    planes, top_count, capacity,
+    part_ref, infos_ref,
+    out_ref,
+    taken, merged, foreign, rise_in, rise_out, fall_in, fall_out,
+    core_send, core_recv, x_send, x_recv, line_send, line_recv,
+):
+    here = lax.axis_index("ea")
+    plane = here // PLANE
+    mine = here // EXPERT_SPLIT
+    partner = here + 1 - 2 * (here % 2)
+    beside = here + 2 - 4 * ((here // 2) % 2)
+    theirs = beside // EXPERT_SPLIT
+    rise_in[plane] = jnp.zeros_like(rise_in[plane])
+    fall_in[plane] = jnp.zeros_like(fall_in[plane])
+    greet(here, plane, planes)
+
+    def core_copy(slot):
+        return remote(
+            part_ref.at[2 * planes + slot], taken.at[slot], core_send.at[slot], core_recv.at[slot],
+            partner,
+        )
+
+    def x_copy(at):
+        return remote(
+            merged.at[planes + at], foreign.at[at], x_send.at[at], x_recv.at[at], beside
+        )
+
+    def line_copy(at, way):
+        out, into = (rise_out, rise_in) if way == 0 else (fall_out, fall_in)
+        return remote(
+            out.at[at], into.at[at], line_send.at[way, at], line_recv.at[way, at],
+            here + (PLANE if way == 0 else -PLANE),
+        )
+
+    def each(body):
+        for d in range(planes - 1, 0, -1):
+            @pl.when(plane + d < planes)
+            def _():
+                body(plane + d, 0)
+
+            @pl.when(plane >= d)
+            def _():
+                body(plane - d, 1)
+
+        body(plane, 2)
+
+    def send_core(at, way):
+        core_copy(planes + at).start()
+        core_copy(at).start()
+
+    def add(slot):
+        core_copy(slot).wait_recv()
+        merged[slot] = (
+            part_ref[slot].astype(jnp.float32) + taken[slot].astype(jnp.float32)
+        ).astype(jnp.bfloat16)
+
+    def send_x(at, way):
+        add(planes + at)
+        x_copy(at).start()
+        add(at)
+
+    def finish(at, way):
+        info = infos_ref[at]
+        x_copy(at).wait_recv()
+        term = 0.0
+        for expert, rows in ((mine, merged), (theirs, foreign)):
+            pick, weight = picks_of(info, expert, top_count, capacity)
+            spread = lax.dot_general(
+                jnp.where(pick, 1.0, 0.0).astype(jnp.bfloat16),
+                rows[at],
+                (((0,), (0,)), ((), ())),
+                preferred_element_type=jnp.float32,
+            )
+            column = jnp.transpose(jnp.broadcast_to(weight, (8, weight.shape[1])))[:, :1]
+            term = term + column * spread
+        if way == 2:
+            rise_out[at] = term.astype(jnp.bfloat16)
+            total = term
+
+            @pl.when(plane > 0)
+            def _():
+                line_copy(at, 0).wait_recv()
+
+            @pl.when(plane < planes - 1)
+            def _():
+                line_copy(at, 1).wait_recv()
+
+            risen = jnp.where(plane > 0, rise_in[at].astype(jnp.float32), 0.0)
+            fallen = jnp.where(plane < planes - 1, fall_in[at].astype(jnp.float32), 0.0)
+            out_ref[...] = (total + risen + fallen).astype(out_ref.dtype)
+        else:
+            out, into = (rise_out, rise_in) if way == 0 else (fall_out, fall_in)
+            inner = plane > 0 if way == 0 else plane < planes - 1
+
+            @pl.when(inner)
+            def _():
+                line_copy(at, way).wait_recv()
+                out[at] = (term + into[at].astype(jnp.float32)).astype(jnp.bfloat16)
+
+            @pl.when(jnp.logical_not(inner))
+            def _():
+                out[at] = term.astype(jnp.bfloat16)
+
+            line_copy(at, way).start()
+
+    each(send_core)
+    each(send_x)
+    each(finish)
+    for at in range(planes):
+        x_copy(at).wait_send()
+
+        @pl.when(plane < at)
+        def _():
+            line_copy(at, 0).wait_send()
+
+        @pl.when(plane > at)
+        def _():
+            line_copy(at, 1).wait_send()
+
+    for slot in range(2 * planes):
+        core_copy(slot).wait_send()
+
+
+def line_local(
     tokens,
     expert_choice_index,
     router_gate_weight,
@@ -149,32 +472,41 @@
 ):
     devices = lax.axis_size("ea")
     experts = devices // EXPERT_SPLIT
+    planes = devices // PLANE
     tok_rows, model_width = tokens.shape
     top_count = expert_choice_index.shape[1]
     capacity = 9 * tok_rows * top_count // (8 * experts)
-    rows_total = devices * capacity
-    mine = lax.axis_index("ea") // EXPERT_SPLIT
+    capacity = -(-capacity // 16) * 16
     block_width = down_weight.shape[1]
     adapter_a = adapter_input_projection
     gate_up_weight, down_w, adapter_out = gate_up_matrix[0], down_weight[0], adapter_output_projection[0]
-
-    choice = lax.all_gather(
-        jnp.concatenate([expert_choice_index.astype(jnp.float32), router_gate_weight], axis=1), "ea"
-    )
-    all_tokens = lax.all_gather(tokens, "ea")
-    all_cotangent = lax.all_gather(cotangent, "ea")
-    named = choice[:, :, :top_count].astype(jnp.int32) == mine
-    weight = jnp.sum(jnp.where(named, choice[:, :, top_count:], 0.0), axis=2)
-    chosen = jnp.any(named, axis=2)
-    place = jnp.cumsum(chosen.astype(jnp.int32), axis=1) - 1
-    place = jnp.where(chosen, place, capacity)
-    pick = place[:, None, :] == jnp.arange(capacity, dtype=jnp.int32)[None, :, None]
-    select = pick.astype(jnp.bfloat16)
-    row_weight = jnp.sum(jnp.where(pick, weight[:, None, :], 0.0), axis=2)
-
-    input_rows = jnp.einsum(
-        "sct,std->scd", select, all_tokens, preferred_element_type=jnp.bfloat16
-    ).reshape(rows_total, model_width)
+    info = jnp.concatenate([expert_choice_index.T.astype(jnp.float32), router_gate_weight.T], axis=0)
+    vmem = pl.BlockSpec(memory_space=pltpu.VMEM)
+    anyspace = pl.BlockSpec(memory_space=pl.ANY)
+    dma = pltpu.SemaphoreType.DMA
+    rows_type = jax.ShapeDtypeStruct((4 * planes, capacity, model_width), jnp.bfloat16)
+    input_rows, gradient_rows, infos = pl.pallas_call(
+        functools.partial(gather_kernel, planes, top_count, capacity),
+        out_shape=(
+            rows_type, rows_type, jax.ShapeDtypeStruct((planes,) + info.shape, jnp.float32)
+        ),
+        in_specs=[anyspace, anyspace, vmem],
+        out_specs=(vmem, vmem, vmem),
+        scratch_shapes=[
+            pltpu.VMEM((2, planes, tok_rows, model_width), jnp.bfloat16),
+            pltpu.VMEM((planes,) + info.shape, jnp.float32),
+            pltpu.VMEM((2, planes, capacity, model_width), jnp.bfloat16),
+            dma((2,)), dma((2, 2, planes)), dma((2, planes)), dma((2, planes)), dma((planes,)),
+            dma((2, planes)), dma((2, planes)), dma((2, 2 * planes)), dma((2, 2 * planes)),
+        ],
+        compiler_params=pltpu.CompilerParams(
+            collective_id=0, has_side_effects=True, vmem_limit_bytes=40 * 2**20
+        ),
+        name="gather_rows",
+    )(tokens, cotangent, info)
+    input_rows = input_rows.reshape(-1, model_width)
+    gradient_rows = gradient_rows.reshape(-1, model_width)
+
     adapter_rows = jnp.dot(input_rows, adapter_a, preferred_element_type=jnp.float32).astype(jnp.bfloat16)
     joined = jnp.dot(
         input_rows, gate_up_weight, preferred_element_type=jnp.float32
@@ -184,21 +516,7 @@
     active = gate_part * sigmoid_gate
     hidden = (active * up_part).astype(jnp.bfloat16)
     partial_value = jnp.dot(hidden, down_w, preferred_element_type=jnp.float32).astype(jnp.bfloat16)
-    spread = jnp.einsum(
-        "sct,scd->std",
-        select,
-        partial_value.reshape(devices, capacity, model_width),
-        preferred_element_type=jnp.float32,
-    )
-    term = (weight[:, :, None] * spread).astype(jnp.bfloat16).reshape(devices * tok_rows, model_width)
-    layer_output = lax.psum_scatter(term, "ea", scatter_dimension=0, tiled=True)
-
-    gradient_rows = jnp.einsum(
-        "sct,std->scd", select, all_cotangent, preferred_element_type=jnp.float32
-    )
-    gradient_rows = (
-        (row_weight[:, :, None] * gradient_rows).astype(jnp.bfloat16).reshape(rows_total, model_width)
-    )
+
     down_grad = lax.dot_general(
         gradient_rows, down_w, (((1,), (1,)), ((), ())), preferred_element_type=jnp.float32
     )
@@ -215,9 +533,34 @@
         )
     ).astype(jnp.bfloat16)
     grad_a = lax.dot_general(
-        input_rows, adapter_gradient, (((0,), (0,)), ((), ())), preferred_element_type=jnp.float32
-    )
-    return (layer_output, lax.psum(grad_a, "ea"), lora_b[None])
+        adapter_gradient, input_rows, (((0,), (0,)), ((), ())), preferred_element_type=jnp.float32
+    )
+    block = (tok_rows, model_width)
+    layer_output = pl.pallas_call(
+        functools.partial(return_kernel, planes, top_count, capacity),
+        out_shape=jax.ShapeDtypeStruct(block, jnp.bfloat16),
+        in_specs=[vmem, vmem],
+        out_specs=vmem,
+        scratch_shapes=[
+            pltpu.VMEM((2 * planes, capacity, model_width), jnp.bfloat16),
+            pltpu.VMEM((2 * planes, capacity, model_width), jnp.bfloat16),
+            pltpu.VMEM((planes, capacity, model_width), jnp.bfloat16),
+        ]
+        + [pltpu.VMEM((planes,) + block, jnp.bfloat16)] * 4
+        + [
+            dma((2 * planes,)), dma((2 * planes,)), dma((planes,)), dma((planes,)),
+            dma((2, planes)), dma((2, planes)),
+        ],
+        compiler_params=pltpu.CompilerParams(
+            collective_id=1, has_side_effects=True, vmem_limit_bytes=40 * 2**20
+        ),
+        name="return_rows",
+    )(partial_value.reshape(4 * planes, capacity, model_width), infos)
+    distance = 0
+    while 2**distance < devices:
+        grad_a = grad_a + from_partner(grad_a, "ea", distance)
+        distance += 1
+    return (layer_output, grad_a.T, lora_b[None])
 
 
 def solution(mesh):
@@ -232,11 +575,12 @@
         P("ea", None, None),
     )
     out_specs = (P(("ga", "ea"), None), P("ga", None), P(("ga", "ea"), None, None))
-    few = mesh.shape["ea"] // EXPERT_SPLIT
+    devices = mesh.shape["ea"]
+    square = devices >= 2 * PLANE and devices & (devices - 1) == 0
 
     def chosen(*args):
-        wide = few > 2 * args[1].shape[1]
-        body = local if wide else shared_local
+        few = devices // EXPERT_SPLIT <= 2 * args[1].shape[1]
+        body = line_local if few and square else local
         return jax.shard_map(
             body, mesh=mesh, in_specs=in_specs, out_specs=out_specs, check_vma=False
         )(*args)

time: 392 us -> 190 us (0.48)
  waiting for transfers between devices: 296 us -> 13.4 us
  Pallas kernels: 0 us -> 133 us
  blocking collectives: 23.8 us -> 0 us
  matrix products: 53.8 us -> 35.3 us
  between operations: 13.8 us -> 0.78 us
    pallas_call x0 -> x2, Pallas kernels: none -> 133 us  [the longest x1 84.1 us: line_local(): pl.pallas_call(functools.partial(gather_kernel, planes, top_count, capaci...]
    reduce_scatter x1 -> x0, waiting for transfers between devices: 110 us -> none  [shared_local(): layer_output = lax.psum_scatter(term, 'ea', scatter_dimension=0, tiled=True)]
    all_gather x2 -> x0, waiting for transfers between devices: 109 us -> none  [the longest x1 56.6 us: shared_local(): all_cotangent = lax.all_gather(cotangent, 'ea')]
    psum x1 -> x0, waiting for transfers between devices: 75.3 us -> none  [shared_local(): return (layer_output, lax.psum(grad_a, 'ea'), lora_b[None])]
    all_gather x1 -> x0, blocking collectives: 23.8 us -> none  [shared_local(): lax.all_gather(jnp.concatenate([expert_choice_index.astype(jnp.float32),...]
    dot_general x10 -> x7, matrix products: 53.8 us -> 35.3 us  [the longest x1 8.36 us: line_local(): jnp.dot(input_rows, gate_up_weight, preferred_element_type=jnp.float32)]
    ppermute x0 -> x4, waiting for transfers between devices: none -> 13.4 us  [from_partner(): return lax.ppermute(value, axis, pairs)]
  transfers between devices with their start and end apart: 4 -> 4, of which waited for: 4 -> 3; matrix products, arithmetic and copies ran while one was open for 8% -> 5% of each run, Pallas kernels for 0% -> 26%
where the time goes in v1:
time: 190 us
  Pallas kernels  133 us (70%)
  matrix products  35.3 us (19%)
  waiting for transfers between devices  13.4 us (7%)
  local copies, waits for them, and re-layouts  2.91 us (2%)
  other arithmetic  2.28 us (1%)
  starting transfers between devices  2.07 us (1%)
    pallas_call x1, Pallas kernels, line_local(): pl.pallas_call(functools.partial(gather_kernel, planes, top_count, capaci...  84.1 us
    pallas_call x1, Pallas kernels, line_local(): pl.pallas_call(functools.partial(return_kernel, planes, top_count, capaci...  49.2 us
    ppermute x4, waiting for transfers between devices, from_partner(): return lax.ppermute(value, axis, pairs)  13.4 us
    dot_general x1, matrix products, line_local(): jnp.dot(input_rows, gate_up_weight, preferred_element_type=jnp.float32)  8.36 us
    dot_general x1, matrix products, line_local(): jnp.dot(hidden, down_w, preferred_element_type=jnp.float32)  8.2 us
    dot_general x1, matrix products, line_local(): lax.dot_general(gradient_rows, down_w, (((1,), (1,)), ((), ())), preferre...  7.09 us
    dot_general x1, matrix products, line_local(): lax.dot_general(adapter_gradient, input_rows, (((0,), (0,)), ((), ())), p...  6.63 us
  transfers between devices with their start and end apart: 4, of which 3 were waited for; matrix products, arithmetic and copies ran while one was open for 5% of the time, Pallas kernels for 26%

profile of v1, /device:TPU:0, one launch (start us, length us, event | category | flops | bytes accessed | tf_op | source)
XLA Modules:
  0.0 190.0 jit_solution(12169294188572776748)
XLA Ops:
  0.6 0.0 copy-start
  0.6 0.8 convert_bitcast_fusion
  1.5 0.7 pad_maximum_fusion.5.info_ref
  2.2 1.0 copy-done.2
  3.3 1.0 copy-done.3
  4.3 84.1 %gather_rows.1 = (bf16[16,80,2048]{2,1,0:T(8,128)(2,1)S(1)}, bf16[16,80,2048]{2,1,0:T(8,128)(2,1)S(1)}, f32[4,8,128]{2,1,0:T(8,128)S(1)}) custom-call(bf16[128,2048]{1,0:T(8,128)(2,1)S(1)} %copy-done.2, bf16[128,2048]{1,0:T(8,128)(2,1)S(1)} %copy-done.3, f32[8,128]{1,0:T(8,128)S(1)} %pad_maximum_fusion.5.info_ref), custom_call_target="tpu_custom_call" | custom-call | tf_op jit(solution)/shard_map/gather_rows/pallas_call | solution.py:488
  88.4 2.4 %convolution_convert_fusion.1 = bf16[1280,16]{0,1:T(8,128)(2,1)S(1)} fusion(bf16[1280,2048]{1,0:T(8,128)(2,1)S(1)} %bitcast.33, bf16[2048,16]{0,1:T(8,128)(2,1)} %param.14), kind=kOutput, calls=%fused_computation.18 | convolution fusion | flops 83906560 | bytes 5349376 | tf_op jit(solution)/shard_map/dot_general | solution.py:510
  90.8 0.0 copy-done.6
  90.8 8.4 %fusion.1 = f32[1280,1408]{1,0:T(8,128)S(1)} fusion(bf16[1280,2048]{1,0:T(8,128)(2,1)S(1)} %bitcast.34, bf16[1,2048,1408]{2,1,0:T(8,128)(2,1)S(1)} %copy-done.6), kind=kOutput, calls=%fused_computation.3 | convolution fusion | flops 7381975040 | bytes 18219008 | tf_op jit(solution)/shard_map/dot_general | solution.py:511
  99.2 0.0 copy-done.1
  99.2 0.0 copy-done.5
  99.2 1.1 fusion
  100.3 0.0 copy-start.4
  100.3 0.0 copy-done
  100.4 7.1 %multiply_convert_fusion.1 = (bf16[1280,704]{1,0:T(8,128)(2,1)}, bf16[1280,704]{1,0:T(8,128)(2,1)}) fusion(f32[1280,1408]{1,0:T(8,128)S(1)} %fusion, bf16[1280,2048]{1,0:T(8,128)(2,1)S(1)} %bitcast.37, bf16[1,704,2048]{2,1,0:T(8,128)(2,1)S(1)} %copy-done), kind=kOutput, calls=%fused_computation.6 | convolution fusion | flops 3702702080 | bytes 18939904 | tf_op jit(solution)/shard_map/dot_general | solution.py:520
  107.4 0.0 copy-done.4
  107.4 6.6 %fusion.9 = f32[16,2048]{1,0:T(8,128)S(1)} fusion(bf16[1280,2048]{1,0:T(8,128)(2,1)} %bitcast.35, bf16[1280,704]{1,0:T(8,128)(2,1)} %get-tuple-element.10, bf16[1280,704]{1,0:T(8,128)(2,1)} %get-tuple-element.9, bf16[1,16,1408]{2,1,0:T(8,128)(2,1)S(1)} %copy-done.5), kind=kOutput, calls=%fused_computation.19 | convolution fusion | flops 148807680 | bytes 9023488 | tf_op jit(solution)/shard_map/dot_general | solution.py:535
  114.1 0.4 collective-permute-start
  114.4 1.0 collective-permute-done
  115.5 0.6 collective-permute-start.1
  116.1 5.2 %collective-permute-done.1 = f32[16,2048]{1,0:T(8,128)S(1)} collective-permute-done((f32[16,2048]{1,0:T(8,128)S(1)}, f32[16,2048]{1,0:T(8,128)S(1)}, u32[]{:S(2)}, u32[]{:S(2)}) %collective-permute-start.1) | collective-permute-done | bytes 131104 | tf_op jit(solution)/shard_map/ppermute | solution.py:20
  121.3 0.1 collective-permute-start.2
  121.4 8.2 %convolution_convert_fusion = bf16[1280,2048]{1,0:T(8,128)(2,1)S(1)} fusion(bf16[1,704,2048]{2,1,0:T(8,128)(2,1)S(1)} %copy-done, f32[1280,1408]{1,0:T(8,128)} %copy-done.4), kind=kOutput, calls=%fused_computation.2 | convolution fusion | flops 3699015680 | bytes 15990784 | tf_op jit(solution)/shard_map/dot_general | solution.py:518
  129.6 0.0 copy-start.7
  129.6 0.0 copy-start.8
  129.6 49.2 %return_rows.1 = bf16[128,2048]{1,0:T(8,128)(2,1)S(1)} custom-call(bf16[16,80,2048]{2,1,0:T(8,128)(2,1)S(1)} %bitcast.36, f32[4,8,128]{2,1,0:T(8,128)S(1)} %get-tuple-element.7.infos_ref), custom_call_target="tpu_custom_call" | custom-call | tf_op jit(solution)/shard_map/return_rows/pallas_call | solution.py:539
  178.8 0.0 collective-permute-done.2
  178.9 1.0 collective-permute-start.3
  179.9 1.5 fusion.8
  181.4 7.1 %collective-permute-done.3 = f32[16,2048]{1,0:T(8,128)S(1)} collective-permute-done((f32[16,2048]{1,0:T(8,128)S(1)}, f32[16,2048]{1,0:T(8,128)S(1)}, u32[]{:S(2)}, u32[]{:S(2)}) %collective-permute-start.3) | collective-permute-done | bytes 131104 | tf_op jit(solution)/shard_map/ppermute | solution.py:20
  188.6 0.7 add_bitcast_fusion
  189.2 0.8 copy.15
  (10 shorter events, 0.1 us)
Async XLA Ops:
  0.6 99.7 %copy-start = (bf16[1,704,2048]{2,1,0:T(8,128)(2,1)S(1)}, bf16[1,704,2048]{2,1,0:T(8,128)(2,1)}, u32[]{:S(2)}) copy-start(bf16[1,704,2048]{2,1,0:T(8,128)(2,1)} %param.13) | copy-start | bytes 8650756
  2.2 1.0 copy-start.2
  3.2 1.0 copy-start.3
  4.3 86.5 %copy-start.6 = (bf16[1,2048,1408]{2,1,0:T(8,128)(2,1)S(1)}, bf16[1,2048,1408]{2,1,0:T(8,128)(2,1)}, u32[]{:S(2)}) copy-start(bf16[1,2048,1408]{2,1,0:T(8,128)(2,1)} %param.12) | copy-start | bytes 17301508
  88.4 10.8 %copy-start.1 = (bf16[16,80,2048]{2,1,0:T(8,128)(2,1)}, bf16[16,80,2048]{2,1,0:T(8,128)(2,1)S(1)}, u32[]{:S(2)}) copy-start(bf16[16,80,2048]{2,1,0:T(8,128)(2,1)S(1)} %get-tuple-element.6) | copy-start | bytes 15728644
  90.8 8.4 %copy-start.5 = (bf16[1,16,1408]{2,1,0:T(8,128)(2,1)S(1)}, bf16[1,16,1408]{2,1,0:T(8,128)(2,1)}, u32[]{:S(2)}) copy-start(bf16[1,16,1408]{2,1,0:T(8,128)(2,1)} %param.15) | copy-start | bytes 135172
  100.3 7.1 %copy-start.4 = (f32[1280,1408]{1,0:T(8,128)}, f32[1280,1408]{1,0:T(8,128)S(1)}, u32[]{:S(2)}) copy-start(f32[1280,1408]{1,0:T(8,128)S(1)} %fusion) | copy-start | bytes 21626884
  114.1 1.4 collective-permute-start
  115.5 5.8 %collective-permute-start.1 = (f32[16,2048]{1,0:T(8,128)S(1)}, f32[16,2048]{1,0:T(8,128)S(1)}, u32[]{:S(2)}, u32[]{:S(2)}) collective-permute-start(f32[16,2048]{1,0:T(8,128)S(1)} %add.24), channel_id=1, source_target_pairs={{0,2},{1,3},{2,0},{3,1},{4,6},{5,7},{6,4},{7,5},{8,10},{9,11},{10,... | collective-permute-start | bytes 393224 | tf_op jit(solution)/shard_map/ppermute | solution.py:20
  121.3 57.5 %collective-permute-start.2 = (f32[16,2048]{1,0:T(8,128)S(1)}, f32[16,2048]{1,0:T(8,128)S(1)}, u32[]{:S(2)}, u32[]{:S(2)}) collective-permute-start(f32[16,2048]{1,0:T(8,128)S(1)} %add.25), channel_id=1, source_target_pairs={{0,4},{1,5},{2,6},{3,7},{4,0},{5,1},{6,2},{7,3},{8,12},{9,13},{10,... | collective-permute-start | bytes 393224 | tf_op jit(solution)/shard_map/ppermute | solution.py:20
  129.6 50.3 %copy-start.7 = (bf16[1280,704]{1,0:T(8,128)(2,1)S(1)}, bf16[1280,704]{1,0:T(8,128)(2,1)}, u32[]{:S(2)}) copy-start(bf16[1280,704]{1,0:T(8,128)(2,1)} %get-tuple-element.9) | copy-start | bytes 5406724
  129.6 50.3 %copy-start.8 = (bf16[1280,704]{1,0:T(8,128)(2,1)S(1)}, bf16[1280,704]{1,0:T(8,128)(2,1)}, u32[]{:S(2)}) copy-start(bf16[1280,704]{1,0:T(8,128)(2,1)} %get-tuple-element.10) | copy-start | bytes 5406724
  178.9 9.7 %collective-permute-start.3 = (f32[16,2048]{1,0:T(8,128)S(1)}, f32[16,2048]{1,0:T(8,128)S(1)}, u32[]{:S(2)}, u32[]{:S(2)}) collective-permute-start(f32[16,2048]{1,0:T(8,128)S(1)} %add.26), channel_id=1, source_target_pairs={{0,8},{1,9},{2,10},{3,11},{4,12},{5,13},{6,14},{7,15},{8,0},{9,1},... | collective-permute-start | bytes 393224 | tf_op jit(solution)/shard_map/ppermute | solution.py:20

commit v2 on v1

--- a/solution.py
+++ b/solution.py
@@ -172,7 +172,7 @@
     )
 
 
-def greet(here, plane, planes):
+def greet(here, plane, planes, extra=()):
     barrier = pltpu.get_barrier_semaphore()
 
     def tell(device):
@@ -191,8 +191,10 @@
     def _():
         tell(here + PLANE)
 
+    for device in extra:
+        tell(device)
     ends = jnp.where(plane > 0, 1, 0) + jnp.where(plane < planes - 1, 1, 0)
-    pl.semaphore_wait(barrier, 2 + ends)
+    pl.semaphore_wait(barrier, 2 + len(extra) + ends)
 
 
 def gather_kernel(
@@ -338,10 +340,10 @@
 
 def return_kernel(
     planes, top_count, capacity,
-    part_ref, infos_ref,
-    out_ref,
-    taken, merged, foreign, rise_in, rise_out, fall_in, fall_out,
-    core_send, core_recv, x_send, x_recv, line_send, line_recv,
+    part_ref, infos_ref, grad_ref,
+    out_ref, total_ref,
+    taken, merged, foreign, rise_in, rise_out, fall_in, fall_out, sums, sums_in,
+    core_send, core_recv, x_send, x_recv, line_send, line_recv, grad_send, grad_recv,
 ):
     here = lax.axis_index("ea")
     plane = here // PLANE
@@ -349,9 +351,21 @@
     partner = here + 1 - 2 * (here % 2)
     beside = here + 2 - 4 * ((here // 2) % 2)
     theirs = beside // EXPERT_SPLIT
+    sums[0] = grad_ref[...]
+    stages = sums.shape[0] - 1
+    mates = [here + 2**i - 2 ** (i + 1) * ((here // 2**i) % 2) for i in range(stages)]
     rise_in[plane] = jnp.zeros_like(rise_in[plane])
     fall_in[plane] = jnp.zeros_like(fall_in[plane])
-    greet(here, plane, planes)
+    greet(here, plane, planes, mates[3:])
+
+    def sum_copy(i):
+        return remote(sums.at[i], sums_in.at[i], grad_send.at[i], grad_recv.at[i], mates[i])
+
+    def next_sum(i):
+        sum_copy(i - 1).wait_recv()
+        sums[i] = sums[i - 1] + sums_in[i - 1]
+        if i < stages:
+            sum_copy(i).start()
 
     def core_copy(slot):
         return remote(
@@ -371,8 +385,8 @@
             here + (PLANE if way == 0 else -PLANE),
         )
 
-    def each(body):
-        for d in range(planes - 1, 0, -1):
+    def each(body, least=0, most=planes - 1):
+        for d in range(most, max(least, 1) - 1, -1):
             @pl.when(plane + d < planes)
             def _():
                 body(plane + d, 0)
@@ -381,7 +395,8 @@
             def _():
                 body(plane - d, 1)
 
-        body(plane, 2)
+        if least == 0:
+            body(plane, 2)
 
     def send_core(at, way):
         core_copy(planes + at).start()
@@ -442,9 +457,19 @@
 
             line_copy(at, way).start()
 
+    sum_copy(0).start()
     each(send_core)
+    next_sum(1)
     each(send_x)
-    each(finish)
+    next_sum(2)
+    each(finish, 2)
+    for i in range(3, stages):
+        next_sum(i)
+    each(finish, 0, 1)
+    next_sum(stages)
+    total_ref[...] = sums[stages]
+    for i in range(stages):
+        sum_copy(i).wait_send()
     for at in range(planes):
         x_copy(at).wait_send()
 
@@ -536,11 +561,15 @@
         adapter_gradient, input_rows, (((0,), (0,)), ((), ())), preferred_element_type=jnp.float32
     )
     block = (tok_rows, model_width)
-    layer_output = pl.pallas_call(
+    stages = devices.bit_length() - 1
+    layer_output, grad_a = pl.pallas_call(
         functools.partial(return_kernel, planes, top_count, capacity),
-        out_shape=jax.ShapeDtypeStruct(block, jnp.bfloat16),
-        in_specs=[vmem, vmem],
-        out_specs=vmem,
+        out_shape=(
+            jax.ShapeDtypeStruct(block, jnp.bfloat16),
+            jax.ShapeDtypeStruct(grad_a.shape, jnp.float32),
+        ),
+        in_specs=[vmem, vmem, vmem],
+        out_specs=(vmem, vmem),
         scratch_shapes=[
             pltpu.VMEM((2 * planes, capacity, model_width), jnp.bfloat16),
             pltpu.VMEM((2 * planes, capacity, model_width), jnp.bfloat16),
@@ -548,18 +577,18 @@
         ]
         + [pltpu.VMEM((planes,) + block, jnp.bfloat16)] * 4
         + [
+            pltpu.VMEM((stages + 1,) + grad_a.shape, jnp.float32),
+            pltpu.VMEM((stages,) + grad_a.shape, jnp.float32),
+        ]
+        + [
             dma((2 * planes,)), dma((2 * planes,)), dma((planes,)), dma((planes,)),
-            dma((2, planes)), dma((2, planes)),
+            dma((2, planes)), dma((2, planes)), dma((stages,)), dma((stages,)),
         ],
         compiler_params=pltpu.CompilerParams(
             collective_id=1, has_side_effects=True, vmem_limit_bytes=40 * 2**20
         ),
         name="return_rows",
-    )(partial_value.reshape(4 * planes, capacity, model_width), infos)
-    distance = 0
-    while 2**distance < devices:
-        grad_a = grad_a + from_partner(grad_a, "ea", distance)
-        distance += 1
+    )(partial_value.reshape(4 * planes, capacity, model_width), infos, grad_a)
     return (layer_output, grad_a.T, lora_b[None])
 
 

time: 190 us -> 182 us (0.958)
  waiting for transfers between devices: 13.4 us -> 0 us
  Pallas kernels: 133 us -> 139 us
  starting transfers between devices: 2.07 us -> 0 us
    ppermute x4 -> x0, waiting for transfers between devices: 13.4 us -> none  [from_partner(): return lax.ppermute(value, axis, pairs)]
    pallas_call x1, Pallas kernels: 49.2 us -> 55.3 us  [line_local(): pl.pallas_call(functools.partial(return_kernel, planes, top_count, capaci...]
    dot_general x1, matrix products: 1.54 us -> 3.82 us  [line_local(): lax.dot_general(adapter_rows, joined_gradient, (((0,), (0,)), ((), ())),...]
    dot_general x1, matrix products: 8.2 us -> 6.13 us  [line_local(): jnp.dot(hidden, down_w, preferred_element_type=jnp.float32)]
    ppermute x4 -> x0, starting transfers between devices: 2.07 us -> none  [from_partner(): return lax.ppermute(value, axis, pairs)]
  transfers between devices with their start and end apart: 4 -> 0, of which waited for: 3 -> 0; matrix products, arithmetic and copies ran while one was open for 5% -> 0% of each run, Pallas kernels for 26% -> 0%
where the time goes in v2:
time: 182 us; the launch traced here: 181 us
  Pallas kernels  139 us (76%)
  matrix products  35.5 us (20%)
  local copies, waits for them, and re-layouts  3.56 us (2%)
    pallas_call x1, Pallas kernels, line_local(): pl.pallas_call(functools.partial(gather_kernel, planes, top_count, capaci...  84.1 us
    pallas_call x1, Pallas kernels, line_local(): pl.pallas_call(functools.partial(return_kernel, planes, top_count, capaci...  55.3 us
    dot_general x1, matrix products, line_local(): jnp.dot(input_rows, gate_up_weight, preferred_element_type=jnp.float32)  8.36 us
    dot_general x1, matrix products, line_local(): lax.dot_general(gradient_rows, down_w, (((1,), (1,)), ((), ())), preferre...  7.09 us
    dot_general x1, matrix products, line_local(): lax.dot_general(adapter_gradient, input_rows, (((0,), (0,)), ((), ())), p...  6.63 us
    dot_general x1, matrix products, line_local(): jnp.dot(hidden, down_w, preferred_element_type=jnp.float32)  6.13 us
    dot_general x1, matrix products, line_local(): lax.dot_general(adapter_rows, joined_gradient, (((0,), (0,)), ((), ())),...  3.82 us

profile of v2, /device:TPU:0, one launch (start us, length us, event | category | flops | bytes accessed | tf_op | source)
XLA Modules:
  0.0 180.8 jit_solution(15448219156511996801)
XLA Ops:
  0.6 0.0 copy-start
  0.6 0.8 convert_bitcast_fusion
  1.5 0.7 pad_maximum_fusion.5.info_ref
  2.2 0.0 copy-start.3
  2.2 1.0 copy-done.3
  3.2 0.0 copy-start.4
  3.3 1.0 copy-done.4
  4.3 0.0 copy-start.6
  4.3 84.1 %gather_rows.1 = (bf16[16,80,2048]{2,1,0:T(8,128)(2,1)S(1)}, bf16[16,80,2048]{2,1,0:T(8,128)(2,1)S(1)}, f32[4,8,128]{2,1,0:T(8,128)S(1)}) custom-call(bf16[128,2048]{1,0:T(8,128)(2,1)S(1)} %copy-done.3, bf16[128,2048]{1,0:T(8,128)(2,1)S(1)} %copy-done.4, f32[8,128]{1,0:T(8,128)S(1)} %pad_maximum_fusion.5.info_ref), custom_call_target="tpu_custom_call" | custom-call | tf_op jit(solution)/shard_map/gather_rows/pallas_call | solution.py:513
  88.4 0.0 copy-start.1
  88.4 2.4 %convolution_convert_fusion.1 = bf16[1280,16]{0,1:T(8,128)(2,1)S(1)} fusion(bf16[1280,2048]{1,0:T(8,128)(2,1)S(1)} %bitcast.32, bf16[2048,16]{0,1:T(8,128)(2,1)} %param.14), kind=kOutput, calls=%fused_computation.18 | convolution fusion | flops 83906560 | bytes 5349376 | tf_op jit(solution)/shard_map/dot_general | solution.py:535
  90.8 0.0 copy-done.6
  90.8 0.0 copy-start.5
  90.8 8.4 %fusion.1 = f32[1280,1408]{1,0:T(8,128)S(1)} fusion(bf16[1280,2048]{1,0:T(8,128)(2,1)S(1)} %bitcast.33, bf16[1,2048,1408]{2,1,0:T(8,128)(2,1)S(1)} %copy-done.6), kind=kOutput, calls=%fused_computation.3 | convolution fusion | flops 7381975040 | bytes 18219008 | tf_op jit(solution)/shard_map/dot_general | solution.py:536
  99.2 0.0 copy-done.1
  99.2 0.0 copy-done.5
  99.2 1.1 fusion
  100.3 0.0 copy-done
  100.3 7.1 %multiply_convert_fusion.1 = (bf16[1280,704]{1,0:T(8,128)(2,1)}, bf16[1280,704]{1,0:T(8,128)(2,1)}) fusion(f32[1280,1408]{1,0:T(8,128)S(1)} %fusion, bf16[1280,2048]{1,0:T(8,128)(2,1)S(1)} %bitcast.37, bf16[1,704,2048]{2,1,0:T(8,128)(2,1)S(1)} %copy-done), kind=kOutput, calls=%fused_computation.6 | convolution fusion | flops 3702702080 | bytes 18939904 | tf_op jit(solution)/shard_map/dot_general | solution.py:545
  107.4 6.1 %convolution_convert_fusion = bf16[1280,2048]{1,0:T(8,128)(2,1)} fusion(bf16[1,704,2048]{2,1,0:T(8,128)(2,1)S(1)} %copy-done, f32[1280,1408]{1,0:T(8,128)S(1)} %fusion), kind=kOutput, calls=%fused_computation.2 | convolution fusion | flops 3699015680 | bytes 15990784 | tf_op jit(solution)/shard_map/dot_general | solution.py:543
  113.6 6.6 %fusion.9.grad_ref = f32[16,2048]{1,0:T(8,128)S(1)} fusion(bf16[1280,2048]{1,0:T(8,128)(2,1)} %bitcast.34, bf16[1280,704]{1,0:T(8,128)(2,1)} %get-tuple-element.14, bf16[1280,704]{1,0:T(8,128)(2,1)} %get-tuple-element.13, bf16[1,16,1408]{2,1,0:T(8,128)(2,1)S(1)} %copy-done.5), kind=kOutput, calls=%fused_computation.19 | convolution fusion | flops 148807680 | bytes 9023488 | tf_op jit(solution)/shard_map/dot_general | solution.py:560
  120.2 0.0 copy-start.2
  120.2 3.8 %fusion.8 = f32[1,16,1408]{2,1,0:T(8,128)} fusion(bf16[1280,16]{0,1:T(8,128)(2,1)S(1)} %convolution_convert_fusion.1, bf16[1280,704]{1,0:T(8,128)(2,1)} %get-tuple-element.14, bf16[1280,704]{1,0:T(8,128)(2,1)} %get-tuple-element.13), kind=kOutput, calls=%fused_computation.17 | convolution fusion | flops 64903168 | bytes 3735552 | tf_op jit(solution)/shard_map/dot_general | solution.py:551
  124.0 0.0 copy-done.2
  124.0 55.3 %return_rows.1 = (bf16[128,2048]{1,0:T(8,128)(2,1)S(1)}, f32[16,2048]{1,0:T(8,128)S(1)}) custom-call(bf16[16,80,2048]{2,1,0:T(8,128)(2,1)S(1)} %bitcast.35, f32[4,8,128]{2,1,0:T(8,128)S(1)} %get-tuple-element.9.infos_ref, f32[16,2048]{1,0:T(8,128)S(1)} %fusion.9.grad_ref), custom_call_target="tpu_custom_call" | custom-call | tf_op jit(solution)/shard_map/return_rows/pallas_call | solution.py:565
  179.3 0.8 copy.16
  180.1 0.7 copy.17
Async XLA Ops:
  0.6 99.7 %copy-start = (bf16[1,704,2048]{2,1,0:T(8,128)(2,1)S(1)}, bf16[1,704,2048]{2,1,0:T(8,128)(2,1)}, u32[]{:S(2)}) copy-start(bf16[1,704,2048]{2,1,0:T(8,128)(2,1)} %param.13) | copy-start | bytes 8650756
  2.2 1.0 copy-start.3
  3.2 1.0 copy-start.4
  4.3 86.5 %copy-start.6 = (bf16[1,2048,1408]{2,1,0:T(8,128)(2,1)S(1)}, bf16[1,2048,1408]{2,1,0:T(8,128)(2,1)}, u32[]{:S(2)}) copy-start(bf16[1,2048,1408]{2,1,0:T(8,128)(2,1)} %param.12) | copy-start | bytes 17301508
  88.4 10.8 %copy-start.1 = (bf16[16,80,2048]{2,1,0:T(8,128)(2,1)}, bf16[16,80,2048]{2,1,0:T(8,128)(2,1)S(1)}, u32[]{:S(2)}) copy-start(bf16[16,80,2048]{2,1,0:T(8,128)(2,1)S(1)} %get-tuple-element.8) | copy-start | bytes 15728644
  90.8 8.4 %copy-start.5 = (bf16[1,16,1408]{2,1,0:T(8,128)(2,1)S(1)}, bf16[1,16,1408]{2,1,0:T(8,128)(2,1)}, u32[]{:S(2)}) copy-start(bf16[1,16,1408]{2,1,0:T(8,128)(2,1)} %param.15) | copy-start | bytes 135172
  120.2 3.8 %copy-start.2 = (bf16[1280,2048]{1,0:T(8,128)(2,1)S(1)}, bf16[1280,2048]{1,0:T(8,128)(2,1)}, u32[]{:S(2)}) copy-start(bf16[1280,2048]{1,0:T(8,128)(2,1)} %convolution_convert_fusion) | copy-start | bytes 15728644
